TPU v7x, 512 devices: a whole 4x4x16 slice. The times are simulated.
512 devices in a mesh: chan: 64 (over y_lo, z, core), loc: 8 (over y_hi, x).
Axes of the slice: x: 4, y: 4 (y_hi: 2, y_lo: 2; y = y_hi * 2 + y_lo), z: 16, core: 2. Of those that a mesh axis runs over, the one named last changes fastest.
Arguments:
- pixels: bfloat16 [2048, 256, 256], P('loc', 'chan'), may hold values from -6 to 6
- patch_mask: int32 [2048, 256], P('loc', 'chan'), may hold values 0 or 1
- group_map: int32 [256], replicated, may hold values from 0 to 63, as said below
- embed_weight: bfloat16 [256, 2048], P(None, 'loc'), may hold values from -0.375 to 0.375
- mask_token: bfloat16 [2048], replicated, may hold values from -6 to 6
- chan_embed: bfloat16 [256, 2048], P('chan'), may hold values from -3 to 3
- agg_weight: float32 [256], P('chan'), may hold values from 0.5 to 2
- query_key: bfloat16 [16, 2048], replicated, may hold values from -0.02734375 to 0.02734375
- group_bias: float32 [16, 64], replicated, may hold values from -0.5 to 255
- norm_gain: float32 [2048], replicated, may hold values from 0.25 to 1.75
- head_weight: bfloat16 [2048, 256, 256], P(None, 'chan'), may hold values from -0.125 to 0.125
- head_bias: float32 [256, 256], P('chan'), may hold values from -3 to 3
Outputs:
- rebuilt: bfloat16 [2048, 256, 256], P('loc', 'chan')
Inputs may be any that keep to these rules, and one draw needn't show every extreme that they name: `group_map`: the 4 channels of each bundle (channels k * 4 to k * 4 + 3) name at most two distinct groups.
All inputs are finite; a program needn't handle non-finite values. No bound on the sum of `patch_mask` on one device may be relied on, other than what follows from the above.
Results may differ from a plain program's by a relative error of at most 0.0051.
Values may be sent and summed in bfloat16 or wider, within the bound.
A program may use at most 64 MiB of HBM per device.

v0:
```python
import math
import jax
import jax.numpy as jnp
from jax import lax
from jax.sharding import PartitionSpec as P

C = 256
E = 2048
G = 64
H = 16
BUNDLE = 4


def shards(
    pixels,
    patch_mask,
    group_map,
    embed_weight,
    mask_token,
    chan_embed,
    agg_weight,
    query_key,
    group_bias,
    norm_gain,
    head_weight,
    head_bias,
):
    locs, own_channels, pixel_count = pixels.shape
    peers = lax.axis_size("chan")
    bundled = group_map.reshape(C // BUNDLE, BUNDLE)
    lowest = jnp.min(bundled, axis=1)
    highest = jnp.max(bundled, axis=1)
    slot_group = jnp.stack([lowest, highest], axis=1)
    me = lax.axis_index("chan")
    own = lax.dynamic_slice_in_dim(bundled, me, 1, 0)[0]
    own_slot = (own != jnp.min(own)).astype(jnp.int32)
    choose = own_slot[None, :] == jnp.arange(2)[:, None]
    loc_peers = lax.axis_size("loc")
    copies = lax.all_to_all(
        jnp.broadcast_to(embed_weight[None], (loc_peers, *embed_weight.shape)),
        "loc",
        0,
        0,
        tiled=True,
    )
    weight = jnp.moveaxis(copies, 0, 1).reshape(pixel_count, E)
    projected = jnp.dot(
        pixels.reshape(locs * own_channels, pixel_count), weight, preferred_element_type=jnp.float32
    ).reshape(locs, own_channels, E)
    hidden = (patch_mask == 1)[:, :, None]
    pre = jnp.where(hidden, mask_token.astype(jnp.float32)[None, None], projected)
    pre = pre + chan_embed.astype(jnp.float32)[None]
    weighted = (
        pre * (1.0 + lax.erf(pre * (1.0 / math.sqrt(2.0)))) * (0.5 * agg_weight)[None, :, None]
    )
    weighted = weighted.astype(jnp.bfloat16)
    sums = jnp.einsum(
        "lke,sk->sle", weighted, choose.astype(jnp.bfloat16), preferred_element_type=jnp.float32
    ).astype(jnp.bfloat16)
    part = jnp.einsum("sle,he->slh", sums, query_key, preferred_element_type=jnp.float32)
    part = part.reshape(2, locs * H)
    every = lax.all_gather(part, "chan", axis=0, tiled=True)
    to_group = (jnp.arange(G)[:, None] == slot_group.reshape(-1)[None]).astype(jnp.float32)
    scores = jnp.dot(to_group, every, precision=lax.Precision.HIGHEST).reshape(G, locs, H)
    scores = scores + group_bias.T[:, None, :]
    attn = jax.nn.softmax(scores, axis=0)
    own_group = jnp.stack([jnp.min(own), jnp.max(own)])
    own_attn = jnp.take(attn, own_group, axis=0)
    pooled = (sums.reshape(2, locs, H, E // H) * own_attn[..., None]).sum(0).reshape(locs, E)
    pooled = lax.psum_scatter(pooled, "chan", scatter_dimension=0, tiled=True)
    inverse = lax.rsqrt(jnp.mean(pooled * pooled, axis=-1, keepdims=True) + 1e-06)
    joined = (pooled * inverse * norm_gain[None]).astype(jnp.bfloat16)
    joined = lax.all_gather(joined, "chan", axis=0, tiled=True)
    decoded = jnp.dot(
        joined,
        head_weight.reshape(E, own_channels * pixel_count),
        preferred_element_type=jnp.float32,
    )
    decoded = decoded + head_bias.reshape(1, own_channels * pixel_count)
    return decoded.astype(jnp.bfloat16).reshape(locs, own_channels, pixel_count)


def solution(mesh):
    return jax.shard_map(
        shards,
        mesh=mesh,
        in_specs=(
            P("loc", "chan", None),
            P("loc", "chan"),
            P(),
            P(None, "loc"),
            P(),
            P("chan", None),
            P("chan"),
            P(),
            P(),
            P(),
            P(None, "chan", None),
            P("chan", None),
        ),
        out_specs=P("loc", "chan", None),
        check_vma=False,
    )
```

profile of v0, /device:TPU:1, one launch (start us, length us, event | category | flops | bytes accessed | tf_op | source)
XLA Modules:
  0.0 764.5 jit_solution(2735376849102494480)
XLA Ops:
  6.5 2.0 broadcast_in_dim.27
  8.6 7.5 all-to-all-start
  16.1 0.8 reshape.155
  16.9 0.7 convert_element_type.27
  17.6 0.7 convert_element_type.26
  20.2 0.7 broadcast_compare_fusion
  20.9 12.3 %all-to-all-done = bf16[8,256,256]{2,1,0:T(8,128)(2,1)S(1)} async-done(((bf16[8,256,256]{2,1,0:T(8,128)(2,1)}), bf16[8,256,256]{2,1,0:T(8,128)(2,1)S(1)}, u32[]{:S(2)}, u32[]{:S(2)}) %all-to-all-start) | async-done | bytes 1048608 | tf_op jit(solution)/shard_map/all_to_all | solution.py:39
  34.4 3.0 multiply_convert_fusion
  37.4 3.0 fusion.2
  40.5 1.4 copy-done.1
  41.8 1.2 fusion.5
  43.1 0.8 reshape.170
  45.1 1.3 fusion.17
  46.4 1.3 compare_and_fusion
  47.7 119.1 %all-gather.5.cloned.1.call-done = f32[64,2,4096]{2,1,0:T(2,128)} async-done(((f32[1,2,4096]{2,1,0:T(2,128)}), f32[64,2,4096]{2,1,0:T(2,128)}) %all-gather.5.cloned.1.call-update) | async-done | bytes 2097168 | tf_op jit(solution)/shard_map/all_gather | solution.py:62
  166.8 2.7 reshape.171
  169.5 2.4 fusion.22
  172.0 1.4 exponential_reduce_fusion
  173.6 1.8 copy.46
  175.5 1.4 copy.48
  178.0 2.6 mul.56
  180.6 5.9 mul.57
  186.5 10.0 %multiply_reduce_fusion = f32[256,2048]{1,0:T(8,128)} fusion(f32[2,256,2048]{2,0,1:T(2,128)} %mul.57, bf16[2,256,2048]{2,0,1:T(2,128)(2,1)S(1)} %copy-done.2), kind=kLoop, calls=%fused_computation.2 | loop fusion | flops 2621440 | bytes 8388608 | tf_op jit(solution)/shard_map/reduce_sum | solution.py:69
  196.8 1.3 dynamic-slice
  198.7 435.7 %all-reduce.3.cloned.1.call-done = f32[256,2048]{1,0:T(8,128)} async-done(((f32[256,2048]{1,0:T(8,128)}), f32[256,2048]{1,0:T(8,128)}) %all-reduce.3.cloned.1.call-update) | async-done | bytes 2097168
  634.4 1.0 multiply_reduce_fusion.1
  635.4 1.5 fusion.11
  637.0 5.2 copy.56
  642.2 109.9 %all-gather.7.cloned.1.call-done = bf16[64,4,2048]{2,1,0:T(4,128)(2,1)} async-done(((bf16[1,4,2048]{2,1,0:T(4,128)(2,1)}), bf16[64,4,2048]{2,1,0:T(4,128)(2,1)}) %all-gather.7.cloned.1.call-update) | async-done | bytes 1048592 | tf_op jit(solution)/shard_map/all_gather | solution.py:73
  752.1 1.3 reshape.173
  753.4 3.4 fusion.7
  756.8 1.2 reshape.160
  (42 shorter events, 6.0 us)
Async XLA Ops:
  6.5 35.3 %copy-start = (bf16[16,2048]{1,0:T(8,128)(2,1)S(1)}, bf16[16,2048]{1,0:T(8,128)(2,1)}, u32[]{:S(2)}) copy-start(bf16[16,2048]{1,0:T(8,128)(2,1)} %param.19) | copy-start | bytes 196612
  6.5 27.9 %copy-start.6 = (bf16[256,4,256]{2,1,0:T(4,128)(2,1)S(1)}, bf16[256,4,256]{2,1,0:T(4,128)(2,1)}, u32[]{:S(2)}) copy-start(bf16[256,4,256]{2,1,0:T(4,128)(2,1)} %param.12) | copy-start | bytes 1572868
  8.6 24.7 %all-to-all-start = ((bf16[8,256,256]{2,1,0:T(8,128)(2,1)}), bf16[8,256,256]{2,1,0:T(8,128)(2,1)S(1)}, u32[]{:S(2)}, u32[]{:S(2)}) async-start(bf16[8,256,256]{2,1,0:T(8,128)(2,1)} %broadcast_in_dim.27), calls=%async_computation | async-start | bytes 2097152 | tf_op jit(solution)/shard_map/all_to_all | solution.py:39
  16.0 150.8 %all-gather.5.cloned.1.call-start = ((), (), s32[]{:S(2)}) async-start(), calls=%async_computation.1 | async-start | bytes 2129920 | tf_op jit(solution)/shard_map/all_gather | solution.py:62
  37.4 6.9 copy-start.3
  40.4 1.4 copy-start.1
  43.9 590.6 %all-reduce.3.cloned.1.call-start = ((), (), s32[]{:S(2)}) async-start(), calls=%async_computation.3 | async-start | bytes 4194304
  180.6 5.9 copy-start.2
  186.5 448.9 %copy-start.4 = (f32[2048]{0:T(1024)S(1)}, f32[2048]{0:T(1024)}, u32[]{:S(2)}) copy-start(f32[2048]{0:T(1024)} %param.21) | copy-start | bytes 24580
  196.5 555.5 %all-gather.7.cloned.1.call-start = ((), (), s32[]{:S(2)}) async-start(), calls=%async_computation.2 | async-start | bytes 1064960 | tf_op jit(solution)/shard_map/all_gather | solution.py:73
  637.0 5.2 copy-start.5
Sparse Core Ops, SparseCore 0:
  44.0 122.8 all-gather.4
  196.7 437.7 all-reduce.2
  637.1 114.9 all-gather.6
where the time goes:
time: 765 us
  waiting for transfers between devices  677 us (88%)
  local copies, waits for them, and re-layouts  31.6 us (4%)
  other arithmetic  21 us (3%)
  between operations  14 us (2%)
  matrix products  13 us (2%)
  starting transfers between devices  7.81 us (1%)
    unnamed x4, waiting for transfers between devices  436 us
    all_gather x1, waiting for transfers between devices, shards(): every = lax.all_gather(part, 'chan', axis=0, tiled=True)  119 us
    all_gather x1, waiting for transfers between devices, shards(): joined = lax.all_gather(joined, 'chan', axis=0, tiled=True)  110 us
  transfers between devices with their start and end apart: 4, of which 4 were waited for; matrix products, arithmetic and copies ran while one was open for 2% of the time, Pallas kernels for 0%

commit v1 on v0

--- a/solution.py
+++ b/solution.py
@@ -70,7 +70,10 @@
     pooled = lax.psum_scatter(pooled, "chan", scatter_dimension=0, tiled=True)
     inverse = lax.rsqrt(jnp.mean(pooled * pooled, axis=-1, keepdims=True) + 1e-06)
     joined = (pooled * inverse * norm_gain[None]).astype(jnp.bfloat16)
-    joined = lax.all_gather(joined, "chan", axis=0, tiled=True)
+    size = lax.axis_size("chan")
+    tiles = jnp.stack([joined for _ in range(size)])
+    tiles = lax.all_to_all(tiles, "chan", split_axis=0, concat_axis=0)
+    joined = jnp.concatenate(tiles, axis=0)
     decoded = jnp.dot(
         joined,
         head_weight.reshape(E, own_channels * pixel_count),

time: 765 us -> 710 us (0.928)
  waiting for transfers between devices: 677 us -> 613 us
    all_gather x1 -> x0, waiting for transfers between devices: 110 us -> none  [shards(): joined = lax.all_gather(joined, 'chan', axis=0, tiled=True)]
    all_to_all x0 -> x1, waiting for transfers between devices: none -> 45.1 us  [shards(): tiles = lax.all_to_all(tiles, 'chan', split_axis=0, concat_axis=0)]
    unnamed x4 -> x3, waiting for transfers between devices: 436 us -> 436 us
where the time goes in v1:
time: 710 us; the launch traced here: 706 us
  waiting for transfers between devices  613 us (86%)
  local copies, waits for them, and re-layouts  32 us (5%)
  other arithmetic  20.4 us (3%)
  between operations  14.3 us (2%)
  starting transfers between devices  13.9 us (2%)
  matrix products  13 us (2%)
    unnamed x3, waiting for transfers between devices  436 us
    all_gather x1, waiting for transfers between devices, shards(): every = lax.all_gather(part, 'chan', axis=0, tiled=True)  119 us
    all_to_all x1, waiting for transfers between devices, shards(): tiles = lax.all_to_all(tiles, 'chan', split_axis=0, concat_axis=0)  45.1 us
  transfers between devices with their start and end apart: 4, of which 4 were waited for; matrix products, arithmetic and copies ran while one was open for 2% of the time, Pallas kernels for 0%

profile of v1, /device:TPU:1, one launch (start us, length us, event | category | flops | bytes accessed | tf_op | source)
XLA Modules:
  0.0 706.2 jit_solution(5124682912213723581)
XLA Ops:
  6.5 2.0 broadcast_in_dim.27
  8.6 7.5 %all-to-all-start = ((bf16[8,256,256]{2,1,0:T(8,128)(2,1)}), bf16[8,256,256]{2,1,0:T(8,128)(2,1)S(1)}, u32[]{:S(2)}, u32[]{:S(2)}) async-start(bf16[8,256,256]{2,1,0:T(8,128)(2,1)} %broadcast_in_dim.27), calls=%async_computation | async-start | bytes 2097152 | tf_op jit(solution)/shard_map/all_to_all | solution.py:39
  16.1 0.8 reshape.160
  16.9 0.7 convert_element_type.27
  20.2 0.7 broadcast_compare_fusion
  20.9 12.3 %all-to-all-done = bf16[8,256,256]{2,1,0:T(8,128)(2,1)S(1)} async-done(((bf16[8,256,256]{2,1,0:T(8,128)(2,1)}), bf16[8,256,256]{2,1,0:T(8,128)(2,1)S(1)}, u32[]{:S(2)}, u32[]{:S(2)}) %all-to-all-start) | async-done | bytes 1048608 | tf_op jit(solution)/shard_map/all_to_all | solution.py:39
  34.4 3.0 multiply_convert_fusion
  37.4 3.0 fusion.2
  40.5 1.4 copy-done.1
  41.8 1.2 fusion.5
  43.1 0.8 reshape.176
  45.1 1.3 fusion.16
  46.4 1.3 compare_and_fusion
  47.7 119.1 %all-gather.3.cloned.1.call-done = f32[64,2,4096]{2,1,0:T(2,128)} async-done(((f32[1,2,4096]{2,1,0:T(2,128)}), f32[64,2,4096]{2,1,0:T(2,128)}) %all-gather.3.cloned.1.call-update) | async-done | bytes 2097168 | tf_op jit(solution)/shard_map/all_gather | solution.py:62
  166.8 2.7 reshape.177
  169.5 2.3 fusion.21
  172.0 1.4 exponential_reduce_fusion
  173.6 1.8 copy.46
  175.5 1.4 copy.48
  178.0 2.6 mul.56
  180.6 5.9 mul.57
  186.5 10.0 %multiply_reduce_fusion = f32[256,2048]{1,0:T(8,128)} fusion(f32[2,256,2048]{2,0,1:T(2,128)} %mul.57, bf16[2,256,2048]{2,0,1:T(2,128)(2,1)S(1)} %copy-done.2), kind=kLoop, calls=%fused_computation.2 | loop fusion | flops 2621440 | bytes 8388608 | tf_op jit(solution)/shard_map/reduce_sum | solution.py:69
  196.5 1.3 dynamic-slice
  198.5 436.0 %all-reduce.3.cloned.1.call-done = f32[256,2048]{1,0:T(8,128)} async-done(((f32[256,2048]{1,0:T(8,128)}), f32[256,2048]{1,0:T(8,128)}) %all-reduce.3.cloned.1.call-update) | async-done | bytes 2097168
  634.5 1.0 multiply_reduce_fusion.1
  635.5 0.9 multiply_convert_fusion.1
  636.4 1.5 stack.29
  637.9 6.3 all-to-all-start.1
  644.2 5.2 copy.56
  649.4 45.1 %all-to-all-done.1 = bf16[64,4,2048]{2,1,0:T(4,128)(2,1)S(1)} async-done(((bf16[64,4,2048]{2,1,0:T(4,128)(2,1)}), bf16[64,4,2048]{2,1,0:T(4,128)(2,1)S(1)}, u32[]{:S(2)}, u32[]{:S(2)}) %all-to-all-start.1) | async-done | bytes 1048608 | tf_op jit(solution)/shard_map/all_to_all | solution.py:75
  694.8 3.4 fusion.7
  698.2 1.2 reshape.166
  (42 shorter events, 6.7 us)
Async XLA Ops:
  6.5 35.3 %copy-start = (bf16[16,2048]{1,0:T(8,128)(2,1)S(1)}, bf16[16,2048]{1,0:T(8,128)(2,1)}, u32[]{:S(2)}) copy-start(bf16[16,2048]{1,0:T(8,128)(2,1)} %param.19) | copy-start | bytes 196612
  6.5 27.9 %copy-start.6 = (bf16[256,4,256]{2,1,0:T(4,128)(2,1)S(1)}, bf16[256,4,256]{2,1,0:T(4,128)(2,1)}, u32[]{:S(2)}) copy-start(bf16[256,4,256]{2,1,0:T(4,128)(2,1)} %param.12) | copy-start | bytes 1572868
  8.6 24.7 %all-to-all-start = ((bf16[8,256,256]{2,1,0:T(8,128)(2,1)}), bf16[8,256,256]{2,1,0:T(8,128)(2,1)S(1)}, u32[]{:S(2)}, u32[]{:S(2)}) async-start(bf16[8,256,256]{2,1,0:T(8,128)(2,1)} %broadcast_in_dim.27), calls=%async_computation | async-start | bytes 2097152 | tf_op jit(solution)/shard_map/all_to_all | solution.py:39
  16.0 150.8 %all-gather.3.cloned.1.call-start = ((), (), s32[]{:S(2)}) async-start(), calls=%async_computation.2 | async-start | bytes 2129920 | tf_op jit(solution)/shard_map/all_gather | solution.py:62
  37.4 6.9 copy-start.3
  40.4 1.4 copy-start.1
  43.9 590.6 %all-reduce.3.cloned.1.call-start = ((), (), s32[]{:S(2)}) async-start(), calls=%async_computation.3 | async-start | bytes 4194304
  180.6 5.9 copy-start.2
  186.5 449.0 %copy-start.4 = (f32[2048]{0:T(1024)S(1)}, f32[2048]{0:T(1024)}, u32[]{:S(2)}) copy-start(f32[2048]{0:T(1024)} %param.21) | copy-start | bytes 24580
  637.9 56.6 %all-to-all-start.1 = ((bf16[64,4,2048]{2,1,0:T(4,128)(2,1)}), bf16[64,4,2048]{2,1,0:T(4,128)(2,1)S(1)}, u32[]{:S(2)}, u32[]{:S(2)}) async-start(bf16[64,4,2048]{2,1,0:T(4,128)(2,1)} %stack.29), calls=%async_computation.1 | async-start | bytes 2097152 | tf_op jit(solution)/shard_map/all_to_all | solution.py:75
  644.2 5.2 copy-start.5
Sparse Core Ops, SparseCore 0:
  44.0 122.8 all-gather.2
  196.7 437.7 all-reduce.2
